TPU v7x, 32 devices: a whole 2x2x4 slice. The times are simulated.
32 devices in a mesh: seq: 32 (over z, y, x, core).
Axes of the slice: x: 2, y: 2, z: 4, core: 2. Of those that a mesh axis runs over, the one named last changes fastest.
Arguments:
- tokens: bfloat16 [5120, 2048], P('seq'), may hold values from -6 to 6
- cotangent: bfloat16 [5120, 2048], P('seq'), may hold values from -6 to 6
- gate_codes: int32 [5120, 256], P('seq'), may hold values from 256 to 4096, as said below
- lengths: int32 [4], replicated, may hold values from 1 to 2560, 5120 in all
- mixer_gain: bfloat16 [2048], P('seq'), may hold values from 0.099609375 to 1.8984375
- query_weight: bfloat16 [2048, 2048], P('seq'), may hold values from -0.125 to 0.125
- key_weight: bfloat16 [2048, 2048], P('seq'), may hold values from -0.125 to 0.125
- value_weight: bfloat16 [2048, 2048], P('seq'), may hold values from -0.125 to 0.125
- head_gain: bfloat16 [2048], P('seq'), may hold values from 0.099609375 to 1.8984375
- output_weight: bfloat16 [2048, 2048], P('seq'), may hold values from -0.125 to 0.125
- feed_gain: bfloat16 [2048], P('seq'), may hold values from 0.099609375 to 1.8984375
- gate_weight: bfloat16 [2048, 5632], P('seq'), may hold values from -0.125 to 0.125
- up_weight: bfloat16 [2048, 5632], P('seq'), may hold values from -0.125 to 0.125
- down_weight: bfloat16 [2048, 5632], P('seq'), may hold values from -0.078125 to 0.078125
Outputs:
- block_out: bfloat16 [5120, 2048], P('seq')
- input_grad: float32 [5120, 2048], P('seq')
- mixer_gain_grad: float32 [2048], P('seq')
- query_grad: float32 [2048, 2048], P('seq')
- key_grad: float32 [2048, 2048], P('seq')
- value_grad: float32 [2048, 2048], P('seq')
- head_gain_grad: float32 [2048], P('seq')
- output_weight_grad: float32 [2048, 2048], P('seq')
- feed_gain_grad: float32 [2048], P('seq')
- gate_grad: float32 [2048, 5632], P('seq')
- up_grad: float32 [2048, 5632], P('seq')
- down_grad: float32 [2048, 5632], P('seq')
Inputs may be any that keep to these rules, and one draw needn't show every extreme that they name: `gate_codes`: whole numbers, forget-gate logits of each token and each of the 4 x 64 slots, times 256. The 4 sequences lie one after another along the tokens; the lengths add up to 5120 and the longest is exactly 2560.
All inputs are finite; a program needn't handle non-finite values.
Results may differ from a plain program's by a relative error of at most 0.017.
The roundings to bfloat16 on the way count: a program that leaves them out, or rounds other values in their place, can miss the bound.
Values may be sent and summed in bfloat16 or wider, within the bound.
A program may use at most 504 MiB of HBM per device.

v0:
```python
import jax
import jax.numpy as jnp
from jax import lax
from jax.sharding import PartitionSpec as P

HEADS = 4
SLOTS = 64
epsilon = 1e-06
highest = lax.Precision.HIGHEST
contract_last = (((1,), (1,)), ((), ()))
contract_first = (((0,), (0,)), ((), ()))


def entering(shard, axis, combine, identity):
    devices, index = (lax.axis_size(axis), lax.axis_index(axis))
    everything = jax.tree.map(lambda part: lax.all_gather(part, axis), shard)
    start = jax.tree.map(
        lambda part, zero: jnp.broadcast_to(jnp.asarray(zero, part.dtype), part.shape),
        shard,
        identity,
    )

    def entering_step(k, before):
        reached = k < index
        new = combine(before, jax.tree.map(lambda part: part[k], everything))
        return jax.tree.map(lambda a, b: jnp.where(reached, a, b), new, before)

    return lax.fori_loop(0, devices, entering_step, start)


def carried_in(shard, axis, combine, identity):
    devices, index = (lax.axis_size(axis), lax.axis_index(axis))
    everything = jax.tree.map(
        lambda part, kind: lax.all_gather(part.astype(kind), axis),
        shard,
        (jnp.bfloat16, jnp.bfloat16),
    )
    start = jax.tree.map(
        lambda part, zero: jnp.broadcast_to(jnp.asarray(zero, part.dtype), part.shape),
        shard,
        identity,
    )

    def carried_step(k, before):
        at = devices - 1 - k
        reached = at > index
        new = combine(
            before, jax.tree.map(lambda part, own: part[at].astype(own.dtype), everything, shard)
        )
        return jax.tree.map(lambda a, b: jnp.where(reached, a, b), new, before)

    return lax.fori_loop(0, devices, carried_step, start)


def rms_factor(value_rows):
    return lax.rsqrt(jnp.mean(value_rows * value_rows, axis=-1, keepdims=True) + epsilon)


def precise_result(form, left, right):
    return jnp.einsum(form, left, right, precision=highest, preferred_element_type=jnp.float32)


def plain_result(form, left, right):
    return jnp.einsum(form, left, right, preferred_element_type=jnp.float32)


def chain_join(earlier, later):
    return (earlier[0] * later[0], later[0][..., None] * earlier[1] + later[1])


def block_tables(decay, starts):
    count = jnp.cumsum(starts)
    length = decay.shape[0]
    places = jnp.arange(length)
    before = places[:, None] >= places[None, :]
    same = jnp.where(before & (count[:, None] == count[None, :]), 1.0, 0.0).astype(jnp.float32)
    fresh_state = jnp.where(count == 0, 1.0, 0.0).astype(jnp.float32)
    logsum = jnp.cumsum(decay, axis=0)
    growth_factor = jnp.exp(logsum)
    backward_pass = jnp.exp(-logsum) * -jnp.expm1(decay)
    tail = jnp.where(count == count[-1], 1.0, 0.0).astype(jnp.float32)
    weight_matrix = growth_factor[-1][None] * backward_pass * tail[:, None, None]
    carried_state = fresh_state[-1] * growth_factor[-1]
    return (same, fresh_state, growth_factor, backward_pass, weight_matrix, carried_state)


def local(
    tokens,
    cotangent,
    gate_codes,
    lengths,
    mixer_gain,
    query_weight,
    key_weight,
    value_weight,
    head_gain,
    output_weight,
    feed_gain,
    gate_weight,
    up_weight,
    down_weight,
):
    local_rows = tokens.shape[0]
    width = tokens.shape[1]
    head_size = width // HEADS
    hidden_width = gate_weight.shape[1]
    tokens_f = tokens.astype(jnp.float32)
    factor_one = rms_factor(tokens_f)
    normed_one = tokens_f * factor_one
    position = lax.axis_index("seq") * local_rows + jnp.arange(local_rows, dtype=jnp.int32)
    first_token = jnp.cumsum(lengths) - lengths
    starts = jnp.sum(jnp.where(position[:, None] == first_token[None, :], 1, 0), axis=1).astype(
        jnp.int32
    )
    decay = jax.nn.log_sigmoid(gate_codes.astype(jnp.float32) / 256.0).reshape(
        local_rows, HEADS, SLOTS
    )
    same, fresh_state, growth_factor, backward_pass, weight_matrix, carried_state = block_tables(
        decay, starts
    )
    piece_a = lax.all_gather(mixer_gain, "seq", axis=0, tiled=True)
    piece_b = lax.all_gather(head_gain, "seq", axis=0, tiled=True)
    piece_c = lax.all_gather(feed_gain, "seq", axis=0, tiled=True)
    piece_query = lax.all_gather(query_weight, "seq", axis=0, tiled=True)
    piece_key = lax.all_gather(key_weight, "seq", axis=0, tiled=True)
    piece_value = lax.all_gather(value_weight, "seq", axis=0, tiled=True)
    section = (normed_one * piece_a.astype(jnp.float32)[None, :]).astype(jnp.bfloat16)
    normed_b = section
    query_acc = jnp.dot(section, piece_query, preferred_element_type=jnp.float32)
    key_acc = jnp.dot(section, piece_key, preferred_element_type=jnp.float32)
    value_acc = jnp.dot(section, piece_value, preferred_element_type=jnp.float32)
    heads_shape = (local_rows, HEADS, head_size)
    query_rows = query_acc.astype(jnp.bfloat16).reshape(heads_shape)
    key_rows = key_acc.astype(jnp.bfloat16).reshape(heads_shape)
    value_rows = value_acc.astype(jnp.bfloat16).reshape(heads_shape)
    query_float = query_rows.astype(jnp.float32)
    local_state = jnp.concatenate(
        [
            precise_result("oft,ofi->fti", weight_matrix, key_rows.astype(jnp.float32)),
            precise_result("oft,ofi->fti", weight_matrix, value_rows.astype(jnp.float32)),
        ],
        axis=-1,
    )
    unit = jnp.ones_like(carried_state)
    blank = jnp.zeros_like(local_state)
    gain_in, state_in = entering((carried_state, local_state), "seq", chain_join, (unit, blank))
    running_key_state = state_in[..., :head_size]
    running_value_state = state_in[..., head_size:]
    affinity = plain_result("thd,shd->hts", query_rows, key_rows)
    masked_scores = affinity * same[None]
    score_matrix = growth_factor * precise_result(
        "ynf,fye->nye", masked_scores, backward_pass
    ) + growth_factor * fresh_state[:, None, None] * precise_result(
        "egr,gjr->egj", query_float, running_key_state
    )
    probs = jax.nn.softmax(score_matrix, axis=-1)
    lifted = probs * growth_factor
    mixing_matrix = (precise_result("thm,shm->hts", lifted, backward_pass) * same[None]).astype(
        jnp.bfloat16
    )
    entry_point = lifted * fresh_state[:, None, None]
    slot_output = plain_result("via,avj->ivj", mixing_matrix, value_rows) + precise_result(
        "xfj,fjg->xfg", entry_point, running_value_state
    )
    head_factor = rms_factor(slot_output)
    unit_heads = slot_output * head_factor
    head_gain_f = piece_b.astype(jnp.float32).reshape(HEADS, head_size)
    normed_heads = (unit_heads * head_gain_f).astype(jnp.bfloat16).reshape(local_rows, width)
    mixed = jnp.dot(
        normed_heads,
        lax.all_gather(output_weight, "seq", axis=0, tiled=True),
        preferred_element_type=jnp.float32,
    )
    residual = tokens_f + mixed
    factor_two = rms_factor(residual)
    normed_two = residual * factor_two
    feed_input = (normed_two * piece_c.astype(jnp.float32)).astype(jnp.bfloat16)
    pieces = (
        lax.all_gather(gate_weight, "seq", axis=0, tiled=True),
        lax.all_gather(up_weight, "seq", axis=0, tiled=True),
    )
    section = feed_input
    gate = jnp.dot(section, pieces[0], preferred_element_type=jnp.float32)
    upward = jnp.dot(section, pieces[1], preferred_element_type=jnp.float32)
    sigma = jax.nn.sigmoid(gate)
    active = gate * sigma
    hidden = (active * upward).astype(jnp.bfloat16)
    feed_out = lax.dot_general(
        hidden,
        lax.all_gather(down_weight, "seq", axis=0, tiled=True),
        contract_last,
        preferred_element_type=jnp.float32,
    )
    block_out = (residual + feed_out).astype(jnp.bfloat16)
    cotangent_f = cotangent.astype(jnp.float32)
    hidden_grad = jnp.dot(
        cotangent,
        lax.all_gather(down_weight, "seq", axis=0, tiled=True),
        preferred_element_type=jnp.float32,
    )
    gate_back = (hidden_grad * upward * sigma * (1.0 + gate * (1.0 - sigma))).astype(jnp.bfloat16)
    up_back = (hidden_grad * active).astype(jnp.bfloat16)
    pieces = lax.all_gather((gate_weight, up_weight), "seq", axis=0, tiled=True)
    feed_in_grad = lax.dot_general(
        gate_back, pieces[0], contract_last, preferred_element_type=jnp.float32
    ) + lax.dot_general(up_back, pieces[1], contract_last, preferred_element_type=jnp.float32)
    feed_grads = jnp.concatenate([gate_back, up_back], axis=1)
    feed_sums = lax.psum_scatter(
        jnp.concatenate(
            [
                lax.dot_general(
                    feed_input, feed_grads, contract_first, preferred_element_type=jnp.float32
                ),
                lax.dot_general(
                    cotangent, hidden, contract_first, preferred_element_type=jnp.float32
                ),
            ],
            axis=1,
        ),
        "seq",
        scatter_dimension=0,
        tiled=True,
    )
    feed_gain_part = jnp.sum(normed_two * feed_in_grad, axis=0)
    scaled_two = feed_in_grad * piece_c.astype(jnp.float32)
    residual_grad = cotangent_f + factor_two * (
        scaled_two - normed_two * jnp.mean(normed_two * scaled_two, axis=-1, keepdims=True)
    )
    mixed_grad = residual_grad.astype(jnp.bfloat16)
    heads_grad = lax.dot_general(
        mixed_grad,
        lax.all_gather(output_weight, "seq", axis=0, tiled=True),
        contract_last,
        preferred_element_type=jnp.float32,
    ).reshape(heads_shape)
    head_gain_part = jnp.sum(unit_heads * heads_grad, axis=0).reshape(width)
    scaled_heads = heads_grad * head_gain_f
    out_back = (
        head_factor
        * (scaled_heads - unit_heads * jnp.mean(unit_heads * scaled_heads, axis=-1, keepdims=True))
    ).astype(jnp.bfloat16)
    output_backward_float = out_back.astype(jnp.float32)
    mixing_grad = plain_result("thd,shd->hts", out_back, value_rows)
    local_value = plain_result("hts,thd->shd", mixing_matrix, out_back)
    leading_value = precise_result("ixn,ixb->xnb", entry_point, output_backward_float)
    lifted_grad = growth_factor * precise_result(
        "ynf,fye->nye", mixing_grad * same[None], backward_pass
    ) + growth_factor * fresh_state[:, None, None] * precise_result(
        "egr,gjr->egj", output_backward_float, running_value_state
    )
    score_grad = probs * (lifted_grad - jnp.sum(probs * lifted_grad, axis=-1, keepdims=True))
    inner_grad = growth_factor * score_grad
    state_gradient = inner_grad * fresh_state[:, None, None]
    affinity_grad = (precise_result("thm,shm->hts", inner_grad, backward_pass) * same[None]).astype(
        jnp.bfloat16
    )
    leading_key = precise_result("ixn,ixb->xnb", state_gradient, query_float)
    back_state = jnp.concatenate([leading_key, leading_value], axis=-1)
    gain_out, later_grad = carried_in((carried_state, back_state), "seq", chain_join, (unit, blank))
    subsequent_key = later_grad[..., :head_size]
    subsequent_value = later_grad[..., head_size:]
    query_back = (
        (
            plain_result("via,avj->ivj", affinity_grad, key_rows)
            + precise_result("xfj,fjg->xfg", state_gradient, running_key_state)
        )
        .astype(jnp.bfloat16)
        .reshape(local_rows, width)
    )
    key_back = (
        (
            plain_result("hts,thd->shd", affinity_grad, query_rows)
            + precise_result("pzo,zot->pzt", weight_matrix, subsequent_key)
        )
        .astype(jnp.bfloat16)
        .reshape(local_rows, width)
    )
    value_back = (
        (local_value + precise_result("pzo,zot->pzt", weight_matrix, subsequent_value))
        .astype(jnp.bfloat16)
        .reshape(local_rows, width)
    )
    pieces = lax.all_gather((query_weight, key_weight, value_weight), "seq", axis=0, tiled=True)
    mixer_in_grad = (
        lax.dot_general(query_back, pieces[0], contract_last, preferred_element_type=jnp.float32)
        + lax.dot_general(key_back, pieces[1], contract_last, preferred_element_type=jnp.float32)
        + lax.dot_general(value_back, pieces[2], contract_last, preferred_element_type=jnp.float32)
    )
    mixer_gain_part = jnp.sum(normed_one * mixer_in_grad, axis=0)
    scaled_one = mixer_in_grad * piece_a.astype(jnp.float32)
    input_grad = residual_grad + factor_one * (
        scaled_one - normed_one * jnp.mean(normed_one * scaled_one, axis=-1, keepdims=True)
    )
    projection_grads = jnp.concatenate([query_back, key_back, value_back], axis=1)
    mixer_sums = lax.psum_scatter(
        jnp.concatenate(
            [
                lax.dot_general(
                    normed_b, projection_grads, contract_first, preferred_element_type=jnp.float32
                ),
                lax.dot_general(
                    normed_heads, mixed_grad, contract_first, preferred_element_type=jnp.float32
                ),
            ],
            axis=1,
        ),
        "seq",
        scatter_dimension=0,
        tiled=True,
    )
    gain_sums = (
        lax.psum_scatter(mixer_gain_part, "seq", scatter_dimension=0, tiled=True),
        lax.psum_scatter(head_gain_part, "seq", scatter_dimension=0, tiled=True),
        lax.psum_scatter(feed_gain_part, "seq", scatter_dimension=0, tiled=True),
    )
    return (
        block_out,
        input_grad,
        gain_sums[0],
        mixer_sums[:, :width],
        mixer_sums[:, width : 2 * width],
        mixer_sums[:, 2 * width : 3 * width],
        gain_sums[1],
        mixer_sums[:, 3 * width :],
        gain_sums[2],
        feed_sums[:, :hidden_width],
        feed_sums[:, hidden_width : 2 * hidden_width],
        feed_sums[:, 2 * hidden_width :],
    )


def solution(mesh):
    return jax.shard_map(
        local,
        mesh=mesh,
        in_specs=(
            P("seq", None),
            P("seq", None),
            P("seq", None),
            P(),
            P("seq"),
            P("seq", None),
            P("seq", None),
            P("seq", None),
            P("seq"),
            P("seq", None),
            P("seq"),
            P("seq", None),
            P("seq", None),
            P("seq", None),
        ),
        out_specs=(
            P("seq", None),
            P("seq", None),
            P("seq"),
            P("seq", None),
            P("seq", None),
            P("seq", None),
            P("seq"),
            P("seq", None),
            P("seq"),
            P("seq", None),
            P("seq", None),
            P("seq", None),
        ),
        check_vma=False,
    )
```

profile of v0, /device:TPU:14, one launch (start us, length us, event | category | flops | bytes accessed | tf_op | source)
XLA Modules:
  0.0 3828.9 jit_solution(6796610249351785658)
XLA Ops:
  21.5 41.1 %all-reduce.10 = (bf16[2048]{0:T(1024)(128)(2,1)S(1)}, bf16[2048]{0:T(1024)(128)(2,1)S(1)}, bf16[2048]{0:T(1024)(128)(2,1)S(1)}) all-reduce(bf16[2048]{0:T(1024)(128)(2,1)S(1)} %dynamic-update-slice, bf16[2048]{0:T(1024)(128)(2,1)S(1)} %dynamic-update-slice.1, bf16[2048]{0:T(1024)(128)(2,1)S(1)} %dynamic-update-slice.2), channel_id=1, replica_groups=mesh['seq'=32] {'seq'}, use_global_device_ids=true, to_apply=%add.2 | all-reduce | flops 6144 | bytes 24576
  62.9 25.9 all-gather.11.cloned.1.call-done
  94.2 73.6 %all-gather.15.cloned.1.call-done = bf16[2048,2048]{1,0:T(8,128)(2,1)} async-done(((bf16[64,2048]{1,0:T(8,128)(2,1)}), bf16[2048,2048]{1,0:T(8,128)(2,1)}) %all-gather.15.cloned.1.call-update) | async-done | bytes 8388624 | tf_op jit(solution)/shard_map/all_gather | solution.py:125
  177.2 29.9 all_gather.59
  207.2 39.6 %all-gather.13.cloned.1.call-done = bf16[2048,2048]{1,0:T(8,128)(2,1)} async-done(((bf16[64,2048]{1,0:T(8,128)(2,1)}), bf16[2048,2048]{1,0:T(8,128)(2,1)}) %all-gather.13.cloned.1.call-update) | async-done | bytes 8388624 | tf_op jit(solution)/shard_map/all_gather | solution.py:124
  255.5 186.1 %all-gather.27.cloned.1.call-done = f32[128,64,1024]{2,1,0:T(8,128)} async-done(((f32[4,64,1024]{2,1,0:T(8,128)}), f32[128,64,1024]{2,1,0:T(8,128)}) %all-gather.27.cloned.1.call-update) | async-done | bytes 33554448 | tf_op jit(solution)/shard_map/all_gather | solution.py:16
  441.5 48.4 %while.30 = (s32[]{:T(128)}, f32[4,64,1024]{2,1,0:T(8,128)S(1)}, s32[]{:T(128)}, f32[32,4,64]{2,1,0:T(4,128)S(1)}, f32[32,4,64,1024]{3,2,1,0:T(8,128)}, /*index=5*/s32[]{:T(128)}, s32[]{:T(128)}) while((s32[]{:T(128)}, f32[4,64,1024]{2,1,0:T(8,128)S(1)}, s32[]{:T(128)}, f32[32,4,64]{2,1,0:T(4,128)S(1)}, ...), condition=%wide.region_8.9_spmd.clone, body=%wide.region_7.8_spmd.clone.sunk | while | flops 1048580 | bytes 3148913 | solution.py:28
  503.7 18.1 all-gather.17.cloned.1.call-done
  527.3 138.7 %all-gather.19.cloned.1.call-done = bf16[2048,5632]{1,0:T(8,128)(2,1)} async-done(((bf16[64,5632]{1,0:T(8,128)(2,1)}), bf16[2048,5632]{1,0:T(8,128)(2,1)}) %all-gather.19.cloned.1.call-update) | async-done | bytes 23068688 | tf_op jit(solution)/shard_map/all_gather | solution.py:179
  666.0 11.5 fusion.106
  677.5 134.2 %all-gather.21.cloned.1.call-done = bf16[2048,5632]{1,0:T(8,128)(2,1)} async-done(((bf16[64,5632]{1,0:T(8,128)(2,1)}), bf16[2048,5632]{1,0:T(8,128)(2,1)}) %all-gather.21.cloned.1.call-update) | async-done | bytes 23068688 | tf_op jit(solution)/shard_map/all_gather | solution.py:180
  811.7 11.5 fusion.107
  823.2 134.1 %all-gather.23.cloned.1.call-done = bf16[2048,5632]{1,0:T(8,128)(2,1)} async-done(((bf16[64,5632]{1,0:T(8,128)(2,1)}), bf16[2048,5632]{1,0:T(8,128)(2,1)}) %all-gather.23.cloned.1.call-update) | async-done | bytes 23068688 | tf_op jit(solution)/shard_map/all_gather | solution.py:190
  957.3 14.1 multiply_convert_fusion
  971.4 13.7 fusion.108
  985.2 14.3 multiply_reduce_fusion
  1013.5 9.2 broadcast_multiply_fusion
  1025.3 20.3 convolution_bitcast_fusion
  1045.6 33.8 fusion.4
  1079.4 89.9 %pad_maximum_fusion = f32[2048,16896]{1,0:T(8,128)} fusion(f32[2048,5632]{1,0:T(8,128)} %convolution_bitcast_fusion, f32[2048,11264]{1,0:T(8,128)} %fusion.4), kind=kLoop, calls=%fused_computation.8 | loop fusion | flops 34603008 | bytes 276824064 | tf_op jit(solution)/shard_map/concatenate | solution.py:209
  1170.0 32.4 all_gather.68
  1210.2 8.4 fusion.82
  1218.6 44.0 %while.31 = (s32[]{:T(128)}, f32[4,64,1024]{2,1,0:T(8,128)S(1)}, s32[]{:T(128)}, bf16[32,4,64]{2,1,0:T(4,128)(2,1)S(1)}, bf16[32,4,64,1024]{3,2,1,0:T(8,128)(2,1...) while((s32[]{:T(128)}, f32[4,64,1024]{2,1,0:T(8,128)S(1)}, s32[]{:T(128)}, ...), condition=%wide.region_17.18_spmd.clone, body=%wide.region_16.17_spmd.clone.sunk | while | flops 1310984 | bytes 2624175 | solution.py:52
  1269.4 22.3 fusion.10
  1291.7 44.9 %pad_maximum_fusion.1 = f32[2048,8192]{1,0:T(8,128)} fusion(f32[2048,2048]{1,0:T(8,128)} %fusion.82, f32[2048,6144]{1,0:T(8,128)} %fusion.10), kind=kLoop, calls=%fused_computation.9 | loop fusion | flops 16777216 | bytes 134217728 | tf_op jit(solution)/shard_map/concatenate | solution.py:296
  1337.3 7.7 fusion.110
  1344.9 13.7 fusion.9
  1358.6 7.0 convolution_add_fusion.3
  1365.6 8.1 fusion.29
  1373.7 52.3 %all-reduce.9 = (f32[2048]{0:T(1024)S(1)}, f32[2048]{0:T(1024)S(1)}, f32[2048]{0:T(1024)S(1)}) all-reduce(f32[2048]{0:T(1024)S(1)} %get-tuple-element.300, f32[2048]{0:T(1024)S(1)} %bitcast.223, f32[2048]{0:T(1024)S(1)} %copy-done.48), channel_id=3, replica_groups=mesh['seq'=32] {'seq'}, use_global_device_ids=true, to_apply=%region_20.21.clone | all-reduce | flops 6144 | bytes 49152
  1430.6 1676.0 %all-reduce.13.cloned.1.call-done = f32[2048,16896]{1,0:T(8,128)} async-done(((f32[2048,16896]{1,0:T(8,128)}), f32[2048,16896]{1,0:T(8,128)}) %all-reduce.13.cloned.1.call-update) | async-done | bytes 138412048
  3111.7 707.4 %reduce-scatter.2.cloned.1.call-done = f32[64,8192]{1,0:T(8,128)} async-done(((f32[2048,8192]{1,0:T(8,128)}), f32[64,8192]{1,0:T(8,128)}) %reduce-scatter.2.cloned.1.call-update) | async-done | bytes 2097168 | tf_op jit(solution)/shard_map/reduce_scatter | solution.py:295
  (357 shorter events, 191.1 us)
Async XLA Ops:
  7.2 81.7 %all-gather.11.cloned.1.call-start = ((), (), s32[]{:S(2)}) async-start(), calls=%async_computation.1 | async-start | bytes 8650752 | tf_op jit(solution)/shard_map/all_gather | solution.py:126
  7.9 159.9 %all-gather.15.cloned.1.call-start = ((), (), s32[]{:S(2)}) async-start(), calls=%async_computation.3 | async-start | bytes 8650752 | tf_op jit(solution)/shard_map/all_gather | solution.py:125
  8.7 238.1 %all-gather.13.cloned.1.call-start = ((), (), s32[]{:S(2)}) async-start(), calls=%async_computation.2 | async-start | bytes 8650752 | tf_op jit(solution)/shard_map/all_gather | solution.py:124
  9.4 432.1 %all-gather.27.cloned.1.call-start = ((), (), s32[]{:S(2)}) async-start(), calls=%async_computation.10 | async-start | bytes 34603008 | tf_op jit(solution)/shard_map/all_gather | solution.py:16
  18.1 44.6 %copy-start.8 = (bf16[160,2048]{1,0:T(8,128)(2,1)S(1)}, bf16[160,2048]{1,0:T(8,128)(2,1)}, u32[]{:S(2)}) copy-start(bf16[160,2048]{1,0:T(8,128)(2,1)} %param.18) | copy-start | bytes 1966084
  20.7 152.0 %copy-start.16 = (f32[160,4,64]{0,2,1:T(8,128)}, f32[160,4,64]{0,2,1:T(8,128)S(1)}, u32[]{:S(2)}) copy-start(f32[160,4,64]{0,2,1:T(8,128)S(1)} %copy.162) | copy-start | bytes 491524
  62.7 184.1 %copy-start.42 = (f32[2048]{0:T(1024)}, f32[2048]{0:T(1024)S(1)}, u32[]{:S(2)}) copy-start(f32[2048]{0:T(1024)S(1)} %convert_element_type.125) | copy-start | bytes 24580
  62.9 183.8 %copy-start.46 = (f32[160]{0:T(256)}, f32[160]{0:T(256)S(1)}, u32[]{:S(2)}) copy-start(f32[160]{0:T(256)S(1)} %add_rsqrt_fusion.2) | copy-start | bytes 1924
  93.8 405.9 %copy-start.23 = (bf16[160,2048]{1,0:T(8,128)(2,1)}, bf16[160,2048]{1,0:T(8,128)(2,1)S(1)}, u32[]{:S(2)}) copy-start(bf16[160,2048]{1,0:T(8,128)(2,1)S(1)} %convolution_convert_fusion.2) | copy-start | bytes 1966084
  174.3 347.5 %all-gather.17.cloned.1.call-start = ((), (), s32[]{:S(2)}) async-start(), calls=%async_computation.4 | async-start | bytes 8650752 | tf_op jit(solution)/shard_map/all_gather | solution.py:171
  174.9 491.1 %all-gather.19.cloned.1.call-start = ((), (), s32[]{:S(2)}) async-start(), calls=%async_computation.5 | async-start | bytes 23789568 | tf_op jit(solution)/shard_map/all_gather | solution.py:179
  175.4 636.2 %all-gather.21.cloned.1.call-start = ((), (), s32[]{:S(2)}) async-start(), calls=%async_computation.6 | async-start | bytes 23789568 | tf_op jit(solution)/shard_map/all_gather | solution.py:180
  176.2 781.1 %all-gather.23.cloned.1.call-start = ((), (), s32[]{:S(2)}) async-start(), calls=%async_computation.7 | async-start | bytes 23789568 | tf_op jit(solution)/shard_map/all_gather | solution.py:190
  176.9 1041.7 %all-gather.25.cloned.1.call-start = ((), (), s32[]{:S(2)}) async-start(), calls=%async_computation.8 | async-start | bytes 17301504 | tf_op jit(solution)/shard_map/all_gather | solution.py:34
  177.2 835.4 %copy-start.14 = (f32[160,4,64]{0,2,1:T(8,128)}, f32[160,4,64]{0,2,1:T(8,128)S(1)}, u32[]{:S(2)}) copy-start(f32[160,4,64]{0,2,1:T(8,128)S(1)} %copy.160) | copy-start | bytes 491524
  207.2 803.2 %copy-start.34 = (f32[160,160]{1,0:T(8,128)}, f32[160,160]{1,0:T(8,128)S(1)}, u32[]{:S(2)}) copy-start(f32[160,160]{1,0:T(8,128)S(1)} %fusion.89) | copy-start | bytes 307204
  251.8 238.2 %copy-start.20 = (bf16[160,2048]{1,0:T(8,128)(2,1)}, bf16[160,2048]{1,0:T(8,128)(2,1)S(1)}, u32[]{:S(2)}) copy-start(bf16[160,2048]{1,0:T(8,128)(2,1)S(1)} %convolution_convert_fusion.1) | copy-start | bytes 1966084
  490.0 519.6 %copy-start = (f32[4,64,1024]{2,1,0:T(8,128)}, f32[4,64,1024]{2,1,0:T(8,128)S(1)}, u32[]{:S(2)}) copy-start(f32[4,64,1024]{2,1,0:T(8,128)S(1)} %get-tuple-element.238) | copy-start | bytes 3145732
  527.1 472.4 %copy-start.2 = (f32[160,2048]{1,0:T(8,128)}, f32[160,2048]{1,0:T(8,128)S(1)}, u32[]{:S(2)}) copy-start(f32[160,2048]{1,0:T(8,128)S(1)} %get-tuple-element.352) | copy-start | bytes 3932164
  971.4 13.7 copy-start.40
  1013.5 10.3 copy-start.21
  1025.2 2081.3 %all-reduce.13.cloned.1.call-start = ((), (), s32[]{:S(2)}) async-start(), calls=%async_computation.11 | async-start | bytes 276824064
  1025.3 20.3 copy-start.12
  1169.3 33.1 copy-start.15
  1169.3 33.1 copy-start.35
  1169.4 33.1 copy-start.44
  1169.4 33.8 copy-start.33
  1169.4 2649.7 %reduce-scatter.2.cloned.1.call-start = ((), (), s32[]{:S(2)}) async-start(), calls=%async_computation.9 | async-start | bytes 69206016 | tf_op jit(solution)/shard_map/reduce_scatter | solution.py:295
  1218.6 44.0 %copy-start.17 = (f32[160,4,64]{0,2,1:T(8,128)S(1)}, f32[160,4,64]{0,2,1:T(8,128)}, u32[]{:S(2)}) copy-start(f32[160,4,64]{0,2,1:T(8,128)} %copy-done.16) | copy-start | bytes 491524
  1337.3 7.7 copy-start.3
  1344.9 13.7 copy-start.19
  1365.6 8.1 copy-start.48
  (33 other events, 76.5 us)
Sparse Core Ops, SparseCore 0:
  10.9 77.9 all-gather.10
  91.7 76.0 all-gather.14
  170.6 76.0 all-gather.12
  250.0 191.4 all-gather.26
  444.3 77.5 all-gather.16
  524.5 141.4 all-gather.18
  668.8 142.7 all-gather.20
  814.5 142.7 all-gather.22
  1025.3 113.6 all-gather.24
  1169.5 1936.9 all-reduce.12
  3108.9 710.1 reduce-scatter.1
where the time goes:
time: 3840 us; the launch traced here: 3830 us
  waiting for transfers between devices  3140 us (82%)
  other arithmetic  253 us (7%)
  matrix products  233 us (6%)
  blocking collectives  156 us (4%)
    unnamed x12, waiting for transfers between devices  1680 us
    reduce_scatter x1, waiting for transfers between devices, local(): lax.psum_scatter(jnp.concatenate([lax.dot_general(normed_b, projection_gr...  707 us
    all_gather x1, waiting for transfers between devices, entering(): everything = jax.tree.map(lambda part: lax.all_gather(part, axis), shard)  186 us
    all_gather x1, waiting for transfers between devices, local(): lax.all_gather(gate_weight, 'seq', axis=0, tiled=True)  139 us
    all_gather x1, waiting for transfers between devices, local(): lax.all_gather(up_weight, 'seq', axis=0, tiled=True)  134 us
    all_gather x1, waiting for transfers between devices, local(): lax.all_gather(down_weight, 'seq', axis=0, tiled=True)  134 us
    unnamed x2, blocking collectives  93.5 us
    concatenate x1, other arithmetic, local(): jnp.concatenate([lax.dot_general(feed_input, feed_grads, contract_first,...  89.9 us
  transfers between devices with their start and end apart: 11, of which 10 were waited for; matrix products, arithmetic and copies ran while one was open for 11% of the time, Pallas kernels for 0%

commit v1 on v0

--- a/solution.py
+++ b/solution.py
@@ -121,8 +121,13 @@
     piece_a = lax.all_gather(mixer_gain, "seq", axis=0, tiled=True)
     piece_b = lax.all_gather(head_gain, "seq", axis=0, tiled=True)
     piece_c = lax.all_gather(feed_gain, "seq", axis=0, tiled=True)
-    piece_query = lax.all_gather(query_weight, "seq", axis=0, tiled=True)
-    piece_key = lax.all_gather(key_weight, "seq", axis=0, tiled=True)
+    piece_query, piece_key = jnp.split(
+        lax.all_gather(
+            jnp.concatenate([query_weight, key_weight], axis=1), "seq", axis=0, tiled=True
+        ),
+        [query_weight.shape[1]],
+        axis=1,
+    )
     piece_value = lax.all_gather(value_weight, "seq", axis=0, tiled=True)
     section = (normed_one * piece_a.astype(jnp.float32)[None, :]).astype(jnp.bfloat16)
     normed_b = section

time: 3840 us -> 3930 us (1.023)
  waiting for transfers between devices: 3140 us -> 3230 us
    unnamed x12 -> x13, waiting for transfers between devices: 1680 us -> 1810 us
    all_gather x2 -> x3, waiting for transfers between devices: 113 us -> 110 us  [the longest x1 110 us: local(): lax.all_gather(jnp.concatenate([query_weight, key_weight], axis=1), 'seq'...]
  transfers between devices with their start and end apart: 11 -> 12, of which waited for: 10 -> 9; matrix products, arithmetic and copies ran while one was open for 11% -> 11% of each run, Pallas kernels for 0% -> 0%
where the time goes in v1:
time: 3930 us; the launch traced here: 3920 us
  waiting for transfers between devices  3230 us (82%)
  other arithmetic  254 us (6%)
  matrix products  232 us (6%)
  blocking collectives  154 us (4%)
    unnamed x13, waiting for transfers between devices  1810 us
    reduce_scatter x1, waiting for transfers between devices, local(): lax.psum_scatter(jnp.concatenate([lax.dot_general(normed_b, projection_gr...  707 us
    all_gather x1, waiting for transfers between devices, entering(): everything = jax.tree.map(lambda part: lax.all_gather(part, axis), shard)  150 us
    all_gather x1, waiting for transfers between devices, local(): lax.all_gather(gate_weight, 'seq', axis=0, tiled=True)  139 us
    all_gather x1, waiting for transfers between devices, local(): lax.all_gather(down_weight, 'seq', axis=0, tiled=True)  134 us
    all_gather x1, waiting for transfers between devices, local(): lax.all_gather(up_weight, 'seq', axis=0, tiled=True)  134 us
    all_gather x1, waiting for transfers between devices, local(): lax.all_gather(jnp.concatenate([query_weight, key_weight], axis=1), 'seq'...  110 us
    unnamed x2, blocking collectives  92.1 us
  transfers between devices with their start and end apart: 12, of which 9 were waited for; matrix products, arithmetic and copies ran while one was open for 11% of the time, Pallas kernels for 0%

profile of v1, /device:TPU:14, one launch (start us, length us, event | category | flops | bytes accessed | tf_op | source)
XLA Modules:
  0.0 3921.4 jit_solution(3124647416362613008)
XLA Ops:
  19.7 40.9 %all-reduce.10 = (bf16[2048]{0:T(1024)(128)(2,1)S(1)}, bf16[2048]{0:T(1024)(128)(2,1)S(1)}, bf16[2048]{0:T(1024)(128)(2,1)S(1)}) all-reduce(bf16[2048]{0:T(1024)(128)(2,1)S(1)} %dynamic-update-slice, bf16[2048]{0:T(1024)(128)(2,1)S(1)} %dynamic-update-slice.1, bf16[2048]{0:T(1024)(128)(2,1)S(1)} %dynamic-update-slice.2), channel_id=1, replica_groups=mesh['seq'=32] {'seq'}, use_global_device_ids=true, to_apply=%add.2 | all-reduce | flops 6144 | bytes 24576
  60.9 27.7 all-gather.12.cloned.1.call-done
  94.0 110.4 %all-gather.14.cloned.1.call-done = bf16[2048,4096]{1,0:T(8,128)(2,1)} async-done(((bf16[64,4096]{1,0:T(8,128)(2,1)}), bf16[2048,4096]{1,0:T(8,128)(2,1)}) %all-gather.14.cloned.1.call-update) | async-done | bytes 16777232 | tf_op jit(solution)/shard_map/all_gather | solution.py:125
  213.7 30.9 all_gather.59
  253.5 150.0 %all-gather.30.cloned.1.call-done = f32[128,64,1024]{2,1,0:T(8,128)} async-done(((f32[4,64,1024]{2,1,0:T(8,128)}), f32[128,64,1024]{2,1,0:T(8,128)}) %all-gather.30.cloned.1.call-update) | async-done | bytes 33554448 | tf_op jit(solution)/shard_map/all_gather | solution.py:16
  403.4 48.4 %while.30 = (s32[]{:T(128)}, f32[4,64,1024]{2,1,0:T(8,128)S(1)}, s32[]{:T(128)}, f32[32,4,64]{2,1,0:T(4,128)S(1)}, f32[32,4,64,1024]{3,2,1,0:T(8,128)}, /*index=5*/s32[]{:T(128)}, s32[]{:T(128)}) while((s32[]{:T(128)}, f32[4,64,1024]{2,1,0:T(8,128)S(1)}, s32[]{:T(128)}, f32[32,4,64]{2,1,0:T(4,128)S(1)}, ...), condition=%wide.region_8.9_spmd.clone, body=%wide.region_7.8_spmd.clone.sunk | while | flops 1048580 | bytes 3148913 | solution.py:28
  465.6 18.1 all-gather.16.cloned.1.call-done
  489.2 138.7 %all-gather.18.cloned.1.call-done = bf16[2048,5632]{1,0:T(8,128)(2,1)} async-done(((bf16[64,5632]{1,0:T(8,128)(2,1)}), bf16[2048,5632]{1,0:T(8,128)(2,1)}) %all-gather.18.cloned.1.call-update) | async-done | bytes 23068688 | tf_op jit(solution)/shard_map/all_gather | solution.py:184
  627.9 11.4 fusion.116
  639.3 134.1 %all-gather.20.cloned.1.call-done = bf16[2048,5632]{1,0:T(8,128)(2,1)} async-done(((bf16[64,5632]{1,0:T(8,128)(2,1)}), bf16[2048,5632]{1,0:T(8,128)(2,1)}) %all-gather.20.cloned.1.call-update) | async-done | bytes 23068688 | tf_op jit(solution)/shard_map/all_gather | solution.py:185
  773.4 11.5 fusion.117
  784.9 134.2 %all-gather.22.cloned.1.call-done = bf16[2048,5632]{1,0:T(8,128)(2,1)} async-done(((bf16[64,5632]{1,0:T(8,128)(2,1)}), bf16[2048,5632]{1,0:T(8,128)(2,1)}) %all-gather.22.cloned.1.call-update) | async-done | bytes 23068688 | tf_op jit(solution)/shard_map/all_gather | solution.py:195
  919.1 14.1 multiply_convert_fusion
  933.1 13.7 fusion.118
  946.9 14.3 multiply_reduce_fusion
  963.1 6.8 fusion.94
  975.3 9.2 broadcast_multiply_fusion
  988.3 20.2 convolution_bitcast_fusion
  1008.5 33.8 fusion.8
  1042.3 90.3 %pad_maximum_fusion = f32[2048,16896]{1,0:T(8,128)} fusion(f32[2048,5632]{1,0:T(8,128)} %convolution_bitcast_fusion, f32[2048,11264]{1,0:T(8,128)} %fusion.8), kind=kLoop, calls=%fused_computation.8 | loop fusion | flops 34603008 | bytes 276824064 | tf_op jit(solution)/shard_map/concatenate | solution.py:214
  1133.2 30.8 all_gather.69
  1171.9 8.4 fusion.92
  1180.3 43.6 %while.31 = (s32[]{:T(128)}, f32[4,64,1024]{2,1,0:T(8,128)S(1)}, s32[]{:T(128)}, bf16[32,4,64]{2,1,0:T(4,128)(2,1)S(1)}, bf16[32,4,64,1024]{3,2,1,0:T(8,128)(2,1...) while((s32[]{:T(128)}, f32[4,64,1024]{2,1,0:T(8,128)S(1)}, s32[]{:T(128)}, ...), condition=%wide.region_17.18_spmd.clone, body=%wide.region_16.17_spmd.clone.sunk | while | flops 1310984 | bytes 2624175 | solution.py:52
  1230.8 21.1 fusion.20
  1252.0 45.6 %pad_maximum_fusion.1 = f32[2048,8192]{1,0:T(8,128)} fusion(f32[2048,2048]{1,0:T(8,128)} %fusion.92, f32[2048,6144]{1,0:T(8,128)} %fusion.20), kind=kLoop, calls=%fused_computation.9 | loop fusion | flops 16777216 | bytes 134217728 | tf_op jit(solution)/shard_map/concatenate | solution.py:301
  1298.3 7.8 fusion.120
  1306.0 13.7 fusion.19
  1319.8 7.5 convolution_add_fusion.3
  1327.4 7.6 fusion.39
  1335.0 51.2 %all-reduce.9 = (f32[2048]{0:T(1024)S(1)}, f32[2048]{0:T(1024)S(1)}, f32[2048]{0:T(1024)S(1)}) all-reduce(f32[2048]{0:T(1024)S(1)} %get-tuple-element.300, f32[2048]{0:T(1024)S(1)} %bitcast.221, f32[2048]{0:T(1024)S(1)} %copy-done.50), channel_id=3, replica_groups=mesh['seq'=32] {'seq'}, use_global_device_ids=true, to_apply=%region_20.21.clone | all-reduce | flops 6144 | bytes 49152
  1390.7 1808.2 %all-reduce.13.cloned.1.call-done = f32[2048,16896]{1,0:T(8,128)} async-done(((f32[2048,16896]{1,0:T(8,128)}), f32[2048,16896]{1,0:T(8,128)}) %all-reduce.13.cloned.1.call-update) | async-done | bytes 138412048
  3204.0 707.2 %reduce-scatter.2.cloned.1.call-done = f32[64,8192]{1,0:T(8,128)} async-done(((f32[2048,8192]{1,0:T(8,128)}), f32[64,8192]{1,0:T(8,128)}) %reduce-scatter.2.cloned.1.call-update) | async-done | bytes 2097168 | tf_op jit(solution)/shard_map/reduce_scatter | solution.py:300
  (367 shorter events, 183.5 us)
Async XLA Ops:
  7.2 81.4 %all-gather.12.cloned.1.call-start = ((), (), s32[]{:S(2)}) async-start(), calls=%async_computation.1 | async-start | bytes 8650752 | tf_op jit(solution)/shard_map/all_gather | solution.py:131
  7.9 196.5 %all-gather.14.cloned.1.call-start = ((), (), s32[]{:S(2)}) async-start(), calls=%async_computation.2 | async-start | bytes 17301504 | tf_op jit(solution)/shard_map/all_gather | solution.py:125
  9.9 393.6 %all-gather.30.cloned.1.call-start = ((), (), s32[]{:S(2)}) async-start(), calls=%async_computation.11 | async-start | bytes 34603008 | tf_op jit(solution)/shard_map/all_gather | solution.py:16
  16.4 44.3 %copy-start.8 = (bf16[160,2048]{1,0:T(8,128)(2,1)S(1)}, bf16[160,2048]{1,0:T(8,128)(2,1)}, u32[]{:S(2)}) copy-start(bf16[160,2048]{1,0:T(8,128)(2,1)} %param.18) | copy-start | bytes 1966084
  18.9 190.4 %copy-start.16 = (f32[160,4,64]{0,2,1:T(8,128)}, f32[160,4,64]{0,2,1:T(8,128)S(1)}, u32[]{:S(2)}) copy-start(f32[160,4,64]{0,2,1:T(8,128)S(1)} %copy.162) | copy-start | bytes 491524
  60.7 184.0 %copy-start.43 = (f32[2048]{0:T(1024)}, f32[2048]{0:T(1024)S(1)}, u32[]{:S(2)}) copy-start(f32[2048]{0:T(1024)S(1)} %convert_element_type.125) | copy-start | bytes 24580
  60.9 183.7 %copy-start.48 = (f32[160]{0:T(256)}, f32[160]{0:T(256)S(1)}, u32[]{:S(2)}) copy-start(f32[160]{0:T(256)S(1)} %add_rsqrt_fusion.2) | copy-start | bytes 1924
  93.5 368.1 %copy-start.24 = (bf16[160,2048]{1,0:T(8,128)(2,1)}, bf16[160,2048]{1,0:T(8,128)(2,1)S(1)}, u32[]{:S(2)}) copy-start(bf16[160,2048]{1,0:T(8,128)(2,1)S(1)} %convolution_convert_fusion) | copy-start | bytes 1966084
  210.9 272.8 %all-gather.16.cloned.1.call-start = ((), (), s32[]{:S(2)}) async-start(), calls=%async_computation.3 | async-start | bytes 8650752 | tf_op jit(solution)/shard_map/all_gather | solution.py:176
  211.5 416.4 %all-gather.18.cloned.1.call-start = ((), (), s32[]{:S(2)}) async-start(), calls=%async_computation.4 | async-start | bytes 23789568 | tf_op jit(solution)/shard_map/all_gather | solution.py:184
  212.0 561.4 %all-gather.20.cloned.1.call-start = ((), (), s32[]{:S(2)}) async-start(), calls=%async_computation.5 | async-start | bytes 23789568 | tf_op jit(solution)/shard_map/all_gather | solution.py:185
  212.6 706.4 %all-gather.22.cloned.1.call-start = ((), (), s32[]{:S(2)}) async-start(), calls=%async_computation.6 | async-start | bytes 23789568 | tf_op jit(solution)/shard_map/all_gather | solution.py:195
  213.4 966.9 %all-gather.26.cloned.1.call-start = ((), (), s32[]{:S(2)}) async-start(), calls=%async_computation.8 | async-start | bytes 17301504 | tf_op jit(solution)/shard_map/all_gather | solution.py:34
  213.6 760.6 %copy-start.14 = (f32[160,4,64]{0,2,1:T(8,128)}, f32[160,4,64]{0,2,1:T(8,128)S(1)}, u32[]{:S(2)}) copy-start(f32[160,4,64]{0,2,1:T(8,128)S(1)} %copy.160) | copy-start | bytes 491524
  244.7 727.5 %copy-start.35 = (f32[160,160]{1,0:T(8,128)}, f32[160,160]{1,0:T(8,128)S(1)}, u32[]{:S(2)}) copy-start(f32[160,160]{1,0:T(8,128)S(1)} %fusion.99) | copy-start | bytes 307204
  249.7 202.2 %copy-start.21 = (bf16[160,2048]{1,0:T(8,128)(2,1)}, bf16[160,2048]{1,0:T(8,128)(2,1)S(1)}, u32[]{:S(2)}) copy-start(bf16[160,2048]{1,0:T(8,128)(2,1)S(1)} %fusion.13) | copy-start | bytes 1966084
  451.9 519.4 %copy-start = (f32[4,64,1024]{2,1,0:T(8,128)}, f32[4,64,1024]{2,1,0:T(8,128)S(1)}, u32[]{:S(2)}) copy-start(f32[4,64,1024]{2,1,0:T(8,128)S(1)} %get-tuple-element.238) | copy-start | bytes 3145732
  489.0 472.2 %copy-start.2 = (f32[160,2048]{1,0:T(8,128)}, f32[160,2048]{1,0:T(8,128)S(1)}, u32[]{:S(2)}) copy-start(f32[160,2048]{1,0:T(8,128)S(1)} %get-tuple-element.352) | copy-start | bytes 3932164
  933.1 13.7 copy-start.41
  975.2 10.3 copy-start.22
  986.9 311.3 %all-gather.24.cloned.1.call-start = ((), (), s32[]{:S(2)}) async-start(), calls=%async_computation.7 | async-start | bytes 8650752 | tf_op jit(solution)/shard_map/all_gather | solution.py:288
  987.7 332.2 %all-gather.28.cloned.1.call-start = ((), (), s32[]{:S(2)}) async-start(), calls=%async_computation.9 | async-start | bytes 8650752 | tf_op jit(solution)/shard_map/all_gather | solution.py:288
  988.2 2210.6 %all-reduce.13.cloned.1.call-start = ((), (), s32[]{:S(2)}) async-start(), calls=%async_computation.12 | async-start | bytes 276824064
  988.3 20.2 copy-start.12
  1132.6 31.4 copy-start.15
  1132.6 31.4 copy-start.36
  1132.6 31.4 copy-start.45
  1132.7 32.0 copy-start.34
  1132.7 2778.6 %reduce-scatter.2.cloned.1.call-start = ((), (), s32[]{:S(2)}) async-start(), calls=%async_computation.10 | async-start | bytes 69206016 | tf_op jit(solution)/shard_map/reduce_scatter | solution.py:300
  1180.3 43.6 %copy-start.17 = (f32[160,4,64]{0,2,1:T(8,128)S(1)}, f32[160,4,64]{0,2,1:T(8,128)}, u32[]{:S(2)}) copy-start(f32[160,4,64]{0,2,1:T(8,128)} %copy-done.16) | copy-start | bytes 491524
  1229.4 22.6 copy-start.19
  1298.3 7.8 copy-start.3
  (37 other events, 97.3 us)
Sparse Core Ops, SparseCore 0:
  10.9 77.6 all-gather.11
  92.0 112.3 all-gather.13
  211.0 192.4 all-gather.29
  406.2 77.5 all-gather.15
  486.4 141.4 all-gather.17
  630.6 142.7 all-gather.19
  776.2 142.7 all-gather.21
  987.0 113.6 all-gather.25
  1103.6 76.8 all-gather.23
  1183.2 76.0 all-gather.27
  1265.7 1933.0 all-reduce.12
  3201.1 710.1 reduce-scatter.1
